TPU v7x, 32 devices: a whole 2x2x4 slice. The times are simulated.
32 devices in a mesh: tm: 8 (over z, y), head: 4 (over x, core).
Axes of the slice: x: 2, y: 2, z: 4, core: 2. Of those that a mesh axis runs over, the one named last changes fastest.
Arguments:
- queries: bfloat16 [2048, 3072], P('tm', 'head'), may hold values from -6 to 6
- key_input: bfloat16 [2048, 3072], P('tm', 'head'), may hold values from -6 to 6
- values: bfloat16 [2048, 3072], P('tm', 'head'), may hold values from -6 to 6
- query_gain: float32 [128], replicated, may hold values from 0.25 to 1.75
- key_gain: float32 [128], replicated, may hold values from 0.25 to 1.75
- frames: int32 [4], replicated, may hold values from 1 to 8, 16 in all
- frame_rate: int32 [4], replicated, may hold values from 8 to 30
- out_weight: bfloat16 [24, 3072, 128], P('head', 'tm'), may hold values from -0.109375 to 0.109375
Outputs:
- mixed: bfloat16 [2048, 3072], P('tm', 'head')
Inputs may be any that keep to these rules, and one draw needn't show every extreme that they name: The clips' frames, in order, make up all 16 frames; the longest clip has exactly 8 frames.
All inputs are finite; a program needn't handle non-finite values.
Results may differ from a plain program's by a relative error of at most 0.0084.
Values may be sent and summed in bfloat16 or wider, within the bound.
A program may use at most 64 MiB of HBM per device.

v0:
```python
import math

import jax
import jax.numpy as jnp
from jax import lax
from jax.sharding import PartitionSpec as P

GW = 16
WIN = 12
SPAN = 7
FRAME = 128


def shifted(block, axis, distance):
    devices = range(lax.axis_size(axis))
    route = [(i - distance, i) for i in devices if i - distance in devices]
    return lax.ppermute(block, axis, route)


def rope_freqs(width):
    steps = jnp.arange(width // 2, dtype=jnp.float32)
    return jnp.exp(steps * (-2.0 * math.log(10000.0) / width))


def clip_of(token_index, frames):
    ends = jnp.cumsum(frames)
    starts = ends - frames
    frame_global = token_index // FRAME
    inside = (
        (frame_global[:, None] >= starts[None, :]) & (frame_global[:, None] < ends[None, :])
    ).astype(jnp.int32)
    clip_id = jnp.sum(inside * jnp.arange(frames.shape[0], dtype=jnp.int32)[None, :], axis=1)
    return (clip_id, frame_global, inside, starts)


def rotary(token_index, frames, frame_rate, head_size):
    clip_id, frame_global, inside, starts = clip_of(token_index, frames)
    frame_start = jnp.sum(inside * starts[None, :], axis=1)
    rate_token = jnp.sum(inside * frame_rate[None, :], axis=1).astype(jnp.float32)
    in_frame = token_index % FRAME
    time_pos = (frame_global - frame_start).astype(jnp.float32) * 24.0 / rate_token
    row_pos = (in_frame // GW).astype(jnp.float32)
    col_pos = (in_frame % GW).astype(jnp.float32)
    side = head_size // 6 * 2
    depth = head_size - 2 * side
    angles = jnp.concatenate(
        [
            time_pos[:, None] * rope_freqs(depth)[None, :],
            row_pos[:, None] * rope_freqs(side)[None, :],
            col_pos[:, None] * rope_freqs(side)[None, :],
        ],
        axis=1,
    )
    return (clip_id, frame_global, jnp.cos(angles), jnp.sin(angles))


def norm_rotate(rows, gain, cosine, sine):
    values_f = rows.astype(jnp.float32)
    mean_sq = jnp.mean(values_f * values_f, axis=-1, keepdims=True)
    normed = values_f * lax.rsqrt(mean_sq + 1e-06) * gain
    half = rows.shape[-1] // 2
    first, second = (normed[..., :half], normed[..., half:])
    cos_b = cosine[:, None, :]
    sin_b = sine[:, None, :]
    return jnp.concatenate(
        [first * cos_b - second * sin_b, second * cos_b + first * sin_b], axis=-1
    ).astype(jnp.bfloat16)


def per_device(queries, key_input, values, query_gain, key_gain, frames, frame_rate, out_weight):
    row_count = queries.shape[0]
    head_size = query_gain.shape[0]
    head_count = queries.shape[1] // head_size
    position = lax.axis_index("tm")
    own_index = position * row_count + jnp.arange(row_count, dtype=jnp.int32)
    q_clip, q_frame, cos_own, sin_own = rotary(own_index, frames, frame_rate, head_size)
    q_rot = norm_rotate(
        queries.reshape(row_count, head_count, head_size), query_gain, cos_own, sin_own
    )
    k_rot = norm_rotate(
        key_input.reshape(row_count, head_count, head_size), key_gain, cos_own, sin_own
    )
    k_flat = k_rot.reshape(row_count, head_count * head_size)

    def attend(partial_value, key_block, value_block, offset):
        key_index = (position - offset) * row_count + jnp.arange(row_count, dtype=jnp.int32)
        k_clip, k_frame, inside, starts = clip_of(key_index, frames)
        key_valid = key_index >= 0
        key_mask = (
            key_valid[None, :]
            & (k_clip[None, :] == q_clip[:, None])
            & (k_frame[None, :] <= q_frame[:, None])
            & (k_frame[None, :] >= q_frame[:, None] - (WIN - 1))
        )
        numerator, denominator = partial_value
        key_heads = key_block.reshape(row_count, head_count, head_size)
        value_heads = value_block.reshape(row_count, head_count, head_size)
        scores = jnp.einsum(
            "qhe,khe->hqk", q_rot, key_heads, preferred_element_type=jnp.float32
        ) / math.sqrt(head_size)
        probs = jnp.where(key_mask[None, :, :], jnp.exp(scores), 0.0)
        denominator = denominator + jnp.sum(probs, axis=2)
        numerator = numerator + jnp.einsum(
            "hqk,khe->qhe",
            probs.astype(jnp.bfloat16),
            value_heads,
            preferred_element_type=jnp.float32,
        )
        return (numerator, denominator)

    zero_num = jnp.zeros((row_count, head_count, head_size), jnp.float32)
    zero_den = jnp.zeros((head_count, row_count), jnp.float32)
    partial_value = attend((zero_num, zero_den), k_flat, values, 0)
    moving = (k_flat, values)
    for distance in range(1, SPAN):
        moving = shifted((moving[0], moving[1]), "tm", 1)
        partial_value = attend(partial_value, moving[0], moving[1], distance)
    numerator, denominator = partial_value
    attended = (numerator / jnp.transpose(denominator)[:, :, None]).astype(jnp.bfloat16)
    projected = jnp.einsum(
        "qhe,hne->qn",
        attended,
        lax.all_gather(out_weight, "tm", axis=1, tiled=True),
        preferred_element_type=jnp.float32,
    )
    summed = lax.psum_scatter(projected, "head", scatter_dimension=1, tiled=True)
    return summed.astype(jnp.bfloat16)


def solution(mesh):
    in_specs = (
        P("tm", "head"),
        P("tm", "head"),
        P("tm", "head"),
        P(),
        P(),
        P(),
        P(),
        P("head", "tm", None),
    )
    out_specs = P("tm", "head")
    return jax.shard_map(
        per_device, mesh=mesh, in_specs=in_specs, out_specs=out_specs, check_vma=False
    )
```

profile of v0, /device:TPU:0, one launch (start us, length us, event | category | flops | bytes accessed | tf_op | source)
XLA Modules:
  0.0 228.7 jit_solution(17673074253823423717)
XLA Ops:
  6.5 0.7 all-gather.2.cloned.1.call-update
  7.4 1.2 copy.24
  11.2 4.9 %collective-permute-start = (bf16[256,768]{0,1:T(8,128)(2,1)S(1)}, bf16[256,768]{0,1:T(8,128)(2,1)S(1)}, u32[]{:S(2)}, u32[]{:S(2)}) collective-permute-start(bf16[256,768]{0,1:T(8,128)(2,1)S(1)} %bitcast.67), channel_id=1, source_target_pairs={{0,4},{4,8},{8,12},{12,16},{16,20},{20,24},{24,28},{1,5},{5,9},{9,... | collective-permute-start | bytes 1179656 | tf_op jit(solution)/shard_map/ppermute | solution.py:17
  16.3 3.4 %collective-permute-start.1 = (bf16[256,768]{0,1:T(8,128)(2,1)S(1)}, bf16[256,768]{0,1:T(8,128)(2,1)S(1)}, u32[]{:S(2)}, u32[]{:S(2)}) collective-permute-start(bf16[256,768]{0,1:T(8,128)(2,1)S(1)} %copy.26), channel_id=1, source_target_pairs={{0,4},{4,8},{8,12},{12,16},{16,20},{20,24},{24,28},{1,5},{5,9},{9,... | collective-permute-start | bytes 1179656 | tf_op jit(solution)/shard_map/ppermute | solution.py:17
  21.1 0.9 compare_and_fusion
  23.2 6.9 %collective-permute-done = bf16[256,768]{0,1:T(8,128)(2,1)S(1)} collective-permute-done((bf16[256,768]{0,1:T(8,128)(2,1)S(1)}, bf16[256,768]{0,1:T(8,128)(2,1)S(1)}, u32[]{:S(2)}, u32[]{:S(2)}) %collective-permute-start) | collective-permute-done | bytes 393248 | tf_op jit(solution)/shard_map/ppermute | solution.py:17
  30.1 4.4 %collective-permute-start.2 = (bf16[256,768]{0,1:T(8,128)(2,1)S(1)}, bf16[256,768]{0,1:T(8,128)(2,1)S(1)}, u32[]{:S(2)}, u32[]{:S(2)}) collective-permute-start(bf16[256,768]{0,1:T(8,128)(2,1)S(1)} %collective-permute-done), channel_id=1, source_target_pairs={{0,4},{4,8},{8,12},{12,16},{16,20},{20,24},{24,28},{1,5},{5,9},{9,... | collective-permute-start | bytes 1179656 | tf_op jit(solution)/shard_map/ppermute | solution.py:17
  35.1 5.2 %collective-permute-done.1 = bf16[256,768]{0,1:T(8,128)(2,1)S(1)} collective-permute-done((bf16[256,768]{0,1:T(8,128)(2,1)S(1)}, bf16[256,768]{0,1:T(8,128)(2,1)S(1)}, u32[]{:S(2)}, u32[]{:S(2)}) %collective-permute-start.1) | collective-permute-done | bytes 393248 | tf_op jit(solution)/shard_map/ppermute | solution.py:17
  40.3 9.6 %collective-permute-start.3 = (bf16[256,768]{0,1:T(8,128)(2,1)S(1)}, bf16[256,768]{0,1:T(8,128)(2,1)S(1)}, u32[]{:S(2)}, u32[]{:S(2)}) collective-permute-start(bf16[256,768]{0,1:T(8,128)(2,1)S(1)} %collective-permute-done.1), channel_id=1, source_target_pairs={{0,4},{4,8},{8,12},{12,16},{16,20},{20,24},{24,28},{1,5},{5,9},{9,... | collective-permute-start | bytes 1179656 | tf_op jit(solution)/shard_map/ppermute | solution.py:17
  50.3 14.5 %collective-permute-start.4 = (bf16[256,768]{0,1:T(8,128)(2,1)S(1)}, bf16[256,768]{0,1:T(8,128)(2,1)S(1)}, u32[]{:S(2)}, u32[]{:S(2)}) collective-permute-start(bf16[256,768]{0,1:T(8,128)(2,1)S(1)} %collective-permute-done.2), channel_id=1, source_target_pairs={{0,4},{4,8},{8,12},{12,16},{16,20},{20,24},{24,28},{1,5},{5,9},{9,... | collective-permute-start | bytes 1179656 | tf_op jit(solution)/shard_map/ppermute | solution.py:17
  65.4 12.1 %collective-permute-start.5 = (bf16[256,768]{0,1:T(8,128)(2,1)S(1)}, bf16[256,768]{0,1:T(8,128)(2,1)S(1)}, u32[]{:S(2)}, u32[]{:S(2)}) collective-permute-start(bf16[256,768]{0,1:T(8,128)(2,1)S(1)} %collective-permute-done.3), channel_id=1, source_target_pairs={{0,4},{4,8},{8,12},{12,16},{16,20},{20,24},{24,28},{1,5},{5,9},{9,... | collective-permute-start | bytes 1179656 | tf_op jit(solution)/shard_map/ppermute | solution.py:17
  78.0 3.3 %collective-permute-done.4 = bf16[256,768]{0,1:T(8,128)(2,1)S(1)} collective-permute-done((bf16[256,768]{0,1:T(8,128)(2,1)S(1)}, bf16[256,768]{0,1:T(8,128)(2,1)S(1)}, u32[]{:S(2)}, u32[]{:S(2)}) %collective-permute-start.4) | collective-permute-done | bytes 393248 | tf_op jit(solution)/shard_map/ppermute | solution.py:17
  81.2 13.2 %collective-permute-start.6 = (bf16[256,768]{0,1:T(8,128)(2,1)S(1)}, bf16[256,768]{0,1:T(8,128)(2,1)S(1)}, u32[]{:S(2)}, u32[]{:S(2)}) collective-permute-start(bf16[256,768]{0,1:T(8,128)(2,1)S(1)} %collective-permute-done.4), channel_id=1, source_target_pairs={{0,4},{4,8},{8,12},{12,16},{16,20},{20,24},{24,28},{1,5},{5,9},{9,... | collective-permute-start | bytes 1179656 | tf_op jit(solution)/shard_map/ppermute | solution.py:17
  95.0 3.1 %collective-permute-done.5 = bf16[256,768]{0,1:T(8,128)(2,1)S(1)} collective-permute-done((bf16[256,768]{0,1:T(8,128)(2,1)S(1)}, bf16[256,768]{0,1:T(8,128)(2,1)S(1)}, u32[]{:S(2)}, u32[]{:S(2)}) %collective-permute-start.5) | collective-permute-done | bytes 393248 | tf_op jit(solution)/shard_map/ppermute | solution.py:17
  98.1 13.2 %collective-permute-start.7 = (bf16[256,768]{0,1:T(8,128)(2,1)S(1)}, bf16[256,768]{0,1:T(8,128)(2,1)S(1)}, u32[]{:S(2)}, u32[]{:S(2)}) collective-permute-start(bf16[256,768]{0,1:T(8,128)(2,1)S(1)} %collective-permute-done.5), channel_id=1, source_target_pairs={{0,4},{4,8},{8,12},{12,16},{16,20},{20,24},{24,28},{1,5},{5,9},{9,... | collective-permute-start | bytes 1179656 | tf_op jit(solution)/shard_map/ppermute | solution.py:17
  111.7 3.3 %collective-permute-done.6 = bf16[256,768]{0,1:T(8,128)(2,1)S(1)} collective-permute-done((bf16[256,768]{0,1:T(8,128)(2,1)S(1)}, bf16[256,768]{0,1:T(8,128)(2,1)S(1)}, u32[]{:S(2)}, u32[]{:S(2)}) %collective-permute-start.6) | collective-permute-done | bytes 393248 | tf_op jit(solution)/shard_map/ppermute | solution.py:17
  114.9 12.4 %collective-permute-start.8 = (bf16[256,768]{0,1:T(8,128)(2,1)S(1)}, bf16[256,768]{0,1:T(8,128)(2,1)S(1)}, u32[]{:S(2)}, u32[]{:S(2)}) collective-permute-start(bf16[256,768]{0,1:T(8,128)(2,1)S(1)} %collective-permute-done.6), channel_id=1, source_target_pairs={{0,4},{4,8},{8,12},{12,16},{16,20},{20,24},{24,28},{1,5},{5,9},{9,... | collective-permute-start | bytes 1179656 | tf_op jit(solution)/shard_map/ppermute | solution.py:17
  127.9 16.3 %collective-permute-start.9 = (bf16[256,768]{0,1:T(8,128)(2,1)S(1)}, bf16[256,768]{0,1:T(8,128)(2,1)S(1)}, u32[]{:S(2)}, u32[]{:S(2)}) collective-permute-start(bf16[256,768]{0,1:T(8,128)(2,1)S(1)} %collective-permute-done.7), channel_id=1, source_target_pairs={{0,4},{4,8},{8,12},{12,16},{16,20},{20,24},{24,28},{1,5},{5,9},{9,... | collective-permute-start | bytes 1179656 | tf_op jit(solution)/shard_map/ppermute | solution.py:17
  144.6 8.7 %collective-permute-start.10 = (bf16[256,768]{0,1:T(8,128)(2,1)S(1)}, bf16[256,768]{0,1:T(8,128)(2,1)S(1)}, u32[]{:S(2)}, u32[]{:S(2)}) collective-permute-start(bf16[256,768]{0,1:T(8,128)(2,1)S(1)} %collective-permute-done.8), channel_id=1, source_target_pairs={{0,4},{4,8},{8,12},{12,16},{16,20},{20,24},{24,28},{1,5},{5,9},{9,... | collective-permute-start | bytes 1179656 | tf_op jit(solution)/shard_map/ppermute | solution.py:17
  153.9 8.0 %collective-permute-start.11 = (bf16[256,768]{0,1:T(8,128)(2,1)S(1)}, bf16[256,768]{0,1:T(8,128)(2,1)S(1)}, u32[]{:S(2)}, u32[]{:S(2)}) collective-permute-start(bf16[256,768]{0,1:T(8,128)(2,1)S(1)} %collective-permute-done.9), channel_id=1, source_target_pairs={{0,4},{4,8},{8,12},{12,16},{16,20},{20,24},{24,28},{1,5},{5,9},{9,... | collective-permute-start | bytes 1179656 | tf_op jit(solution)/shard_map/ppermute | solution.py:17
  163.0 5.1 %collective-permute-done.11 = bf16[256,768]{0,1:T(8,128)(2,1)S(1)} collective-permute-done((bf16[256,768]{0,1:T(8,128)(2,1)S(1)}, bf16[256,768]{0,1:T(8,128)(2,1)S(1)}, u32[]{:S(2)}, u32[]{:S(2)}) %collective-permute-start.11) | collective-permute-done | bytes 393248 | tf_op jit(solution)/shard_map/ppermute | solution.py:17
  168.1 5.7 %convolution_bitcast_fusion = f32[256,3072]{1,0:T(8,128)} fusion(bf16[6,3072,128]{2,1,0:T(8,128)(2,1)} %all-gather.2.cloned.1.call-done, f32[6,256,128]{2,1,0:T(8,128)S(1)} %convolution_add_fusion.1, bf16[256,6,128]{0,2,1:T(8,128)(2,1)S(1)} %bitcast.79, bf16[6,256,256]{1,2,0:T(8,128)(2,1)S(1)} %get-tuple-element.35, f32[256,6]{0,1:T(8,128)S(1)} %add_bitcast_fusion), kind=kOutput, calls=%fused_computation | convolution fusion | flops 1309212672 | bytes 9836544 | tf_op jit(solution)/shard_map/qhe,hne->qn/dot_general | solution.py:120
  173.8 46.2 %reduce-scatter.2.cloned.1.call-done = f32[256,768]{1,0:T(8,128)} async-done(((f32[256,3072]{1,0:T(8,128)}), f32[256,768]{1,0:T(8,128)}) %reduce-scatter.2.cloned.1.call-update) | async-done | bytes 786448 | tf_op jit(solution)/shard_map/reduce_scatter | solution.py:126
  220.0 1.9 convert_element_type.101
  (71 shorter events, 10.9 us)
Async XLA Ops:
  6.5 2.3 copy-start.5
  6.5 2.5 %copy-start.4 = (s32[4]{0:T(128)S(1)}, s32[4]{0:T(128)}, u32[]{:S(2)}) copy-start(s32[4]{0:T(128)} %param.14) | copy-start | bytes 52
  6.5 161.5 %all-gather.2.cloned.1.call-start = ((), (), s32[]{:S(2)}) async-start(), calls=%async_computation.1 | async-start | bytes 5308416 | tf_op jit(solution)/shard_map/all_gather | solution.py:123
  7.3 212.7 %reduce-scatter.2.cloned.1.call-start = ((), (), s32[]{:S(2)}) async-start(), calls=%async_computation.2 | async-start | bytes 3932160 | tf_op jit(solution)/shard_map/reduce_scatter | solution.py:126
  7.4 2.7 %copy-start.2 = (f32[128]{0:T(128)S(1)}, f32[128]{0:T(128)}, u32[]{:S(2)}) copy-start(f32[128]{0:T(128)} %param.12) | copy-start | bytes 1540
  10.7 5.4 %copy-start = (bf16[256,768]{1,0:T(8,128)(2,1)S(1)}, bf16[256,768]{1,0:T(8,128)(2,1)}, u32[]{:S(2)}) copy-start(bf16[256,768]{1,0:T(8,128)(2,1)} %param.10) | copy-start | bytes 1179652
  10.8 9.0 %copy-start.1 = (bf16[256,768]{1,0:T(8,128)(2,1)S(1)}, bf16[256,768]{1,0:T(8,128)(2,1)}, u32[]{:S(2)}) copy-start(bf16[256,768]{1,0:T(8,128)(2,1)} %param.8) | copy-start | bytes 1179652
  11.2 9.1 %copy-start.3 = (f32[128]{0:T(128)S(1)}, f32[128]{0:T(128)}, u32[]{:S(2)}) copy-start(f32[128]{0:T(128)} %param.11) | copy-start | bytes 1540
  11.2 18.9 %collective-permute-start = (bf16[256,768]{0,1:T(8,128)(2,1)S(1)}, bf16[256,768]{0,1:T(8,128)(2,1)S(1)}, u32[]{:S(2)}, u32[]{:S(2)}) collective-permute-start(bf16[256,768]{0,1:T(8,128)(2,1)S(1)} %bitcast.67), channel_id=1, source_target_pairs={{0,4},{4,8},{8,12},{12,16},{16,20},{20,24},{24,28},{1,5},{5,9},{9,... | collective-permute-start | bytes 1179656 | tf_op jit(solution)/shard_map/ppermute | solution.py:17
  16.3 24.0 %collective-permute-start.1 = (bf16[256,768]{0,1:T(8,128)(2,1)S(1)}, bf16[256,768]{0,1:T(8,128)(2,1)S(1)}, u32[]{:S(2)}, u32[]{:S(2)}) collective-permute-start(bf16[256,768]{0,1:T(8,128)(2,1)S(1)} %copy.26), channel_id=1, source_target_pairs={{0,4},{4,8},{8,12},{12,16},{16,20},{20,24},{24,28},{1,5},{5,9},{9,... | collective-permute-start | bytes 1179656 | tf_op jit(solution)/shard_map/ppermute | solution.py:17
  30.1 20.2 %collective-permute-start.2 = (bf16[256,768]{0,1:T(8,128)(2,1)S(1)}, bf16[256,768]{0,1:T(8,128)(2,1)S(1)}, u32[]{:S(2)}, u32[]{:S(2)}) collective-permute-start(bf16[256,768]{0,1:T(8,128)(2,1)S(1)} %collective-permute-done), channel_id=1, source_target_pairs={{0,4},{4,8},{8,12},{12,16},{16,20},{20,24},{24,28},{1,5},{5,9},{9,... | collective-permute-start | bytes 1179656 | tf_op jit(solution)/shard_map/ppermute | solution.py:17
  40.3 25.1 %collective-permute-start.3 = (bf16[256,768]{0,1:T(8,128)(2,1)S(1)}, bf16[256,768]{0,1:T(8,128)(2,1)S(1)}, u32[]{:S(2)}, u32[]{:S(2)}) collective-permute-start(bf16[256,768]{0,1:T(8,128)(2,1)S(1)} %collective-permute-done.1), channel_id=1, source_target_pairs={{0,4},{4,8},{8,12},{12,16},{16,20},{20,24},{24,28},{1,5},{5,9},{9,... | collective-permute-start | bytes 1179656 | tf_op jit(solution)/shard_map/ppermute | solution.py:17
  50.3 30.9 %collective-permute-start.4 = (bf16[256,768]{0,1:T(8,128)(2,1)S(1)}, bf16[256,768]{0,1:T(8,128)(2,1)S(1)}, u32[]{:S(2)}, u32[]{:S(2)}) collective-permute-start(bf16[256,768]{0,1:T(8,128)(2,1)S(1)} %collective-permute-done.2), channel_id=1, source_target_pairs={{0,4},{4,8},{8,12},{12,16},{16,20},{20,24},{24,28},{1,5},{5,9},{9,... | collective-permute-start | bytes 1179656 | tf_op jit(solution)/shard_map/ppermute | solution.py:17
  65.4 32.6 %collective-permute-start.5 = (bf16[256,768]{0,1:T(8,128)(2,1)S(1)}, bf16[256,768]{0,1:T(8,128)(2,1)S(1)}, u32[]{:S(2)}, u32[]{:S(2)}) collective-permute-start(bf16[256,768]{0,1:T(8,128)(2,1)S(1)} %collective-permute-done.3), channel_id=1, source_target_pairs={{0,4},{4,8},{8,12},{12,16},{16,20},{20,24},{24,28},{1,5},{5,9},{9,... | collective-permute-start | bytes 1179656 | tf_op jit(solution)/shard_map/ppermute | solution.py:17
  81.2 33.7 %collective-permute-start.6 = (bf16[256,768]{0,1:T(8,128)(2,1)S(1)}, bf16[256,768]{0,1:T(8,128)(2,1)S(1)}, u32[]{:S(2)}, u32[]{:S(2)}) collective-permute-start(bf16[256,768]{0,1:T(8,128)(2,1)S(1)} %collective-permute-done.4), channel_id=1, source_target_pairs={{0,4},{4,8},{8,12},{12,16},{16,20},{20,24},{24,28},{1,5},{5,9},{9,... | collective-permute-start | bytes 1179656 | tf_op jit(solution)/shard_map/ppermute | solution.py:17
  98.1 29.8 %collective-permute-start.7 = (bf16[256,768]{0,1:T(8,128)(2,1)S(1)}, bf16[256,768]{0,1:T(8,128)(2,1)S(1)}, u32[]{:S(2)}, u32[]{:S(2)}) collective-permute-start(bf16[256,768]{0,1:T(8,128)(2,1)S(1)} %collective-permute-done.5), channel_id=1, source_target_pairs={{0,4},{4,8},{8,12},{12,16},{16,20},{20,24},{24,28},{1,5},{5,9},{9,... | collective-permute-start | bytes 1179656 | tf_op jit(solution)/shard_map/ppermute | solution.py:17
  114.9 29.7 %collective-permute-start.8 = (bf16[256,768]{0,1:T(8,128)(2,1)S(1)}, bf16[256,768]{0,1:T(8,128)(2,1)S(1)}, u32[]{:S(2)}, u32[]{:S(2)}) collective-permute-start(bf16[256,768]{0,1:T(8,128)(2,1)S(1)} %collective-permute-done.6), channel_id=1, source_target_pairs={{0,4},{4,8},{8,12},{12,16},{16,20},{20,24},{24,28},{1,5},{5,9},{9,... | collective-permute-start | bytes 1179656 | tf_op jit(solution)/shard_map/ppermute | solution.py:17
  127.9 26.0 %collective-permute-start.9 = (bf16[256,768]{0,1:T(8,128)(2,1)S(1)}, bf16[256,768]{0,1:T(8,128)(2,1)S(1)}, u32[]{:S(2)}, u32[]{:S(2)}) collective-permute-start(bf16[256,768]{0,1:T(8,128)(2,1)S(1)} %collective-permute-done.7), channel_id=1, source_target_pairs={{0,4},{4,8},{8,12},{12,16},{16,20},{20,24},{24,28},{1,5},{5,9},{9,... | collective-permute-start | bytes 1179656 | tf_op jit(solution)/shard_map/ppermute | solution.py:17
  144.6 17.8 %collective-permute-start.10 = (bf16[256,768]{0,1:T(8,128)(2,1)S(1)}, bf16[256,768]{0,1:T(8,128)(2,1)S(1)}, u32[]{:S(2)}, u32[]{:S(2)}) collective-permute-start(bf16[256,768]{0,1:T(8,128)(2,1)S(1)} %collective-permute-done.8), channel_id=1, source_target_pairs={{0,4},{4,8},{8,12},{12,16},{16,20},{20,24},{24,28},{1,5},{5,9},{9,... | collective-permute-start | bytes 1179656 | tf_op jit(solution)/shard_map/ppermute | solution.py:17
  153.9 14.1 %collective-permute-start.11 = (bf16[256,768]{0,1:T(8,128)(2,1)S(1)}, bf16[256,768]{0,1:T(8,128)(2,1)S(1)}, u32[]{:S(2)}, u32[]{:S(2)}) collective-permute-start(bf16[256,768]{0,1:T(8,128)(2,1)S(1)} %collective-permute-done.9), channel_id=1, source_target_pairs={{0,4},{4,8},{8,12},{12,16},{16,20},{20,24},{24,28},{1,5},{5,9},{9,... | collective-permute-start | bytes 1179656 | tf_op jit(solution)/shard_map/ppermute | solution.py:17
Sparse Core Ops, SparseCore 0:
  9.6 123.1 all-gather.1
  173.9 46.0 reduce-scatter.1
where the time goes:
time: 229 us
  starting transfers between devices  121 us (53%)
  waiting for transfers between devices  73.8 us (32%)
  between operations  13.9 us (6%)
  matrix products  12.3 us (5%)
  other arithmetic  6.14 us (3%)
    ppermute x12, starting transfers between devices, shifted(): return lax.ppermute(block, axis, route)  121 us
    reduce_scatter x1, waiting for transfers between devices, per_device(): lax.psum_scatter(projected, 'head', scatter_dimension=1, tiled=True)  46.2 us
    ppermute x12, waiting for transfers between devices, shifted(): return lax.ppermute(block, axis, route)  26.8 us
    dot_general x1, matrix products, per_device(): jnp.einsum('qhe,hne->qn', attended, lax.all_gather(out_weight, 'tm', axis...  5.71 us
  transfers between devices with their start and end apart: 14, of which 7 were waited for; matrix products, arithmetic and copies ran while one was open for 6% of the time, Pallas kernels for 0%

commit v1 on v0

v1 whole, which is shorter than its diff:
```python
import functools
import math

import jax
import jax.numpy as jnp
from jax import lax
from jax.experimental import pallas as pl
from jax.experimental.pallas import tpu as pltpu
from jax.sharding import PartitionSpec as P

GW = 16
WIN = 12
FRAME = 128
MESH = pl.DeviceIdType.MESH


def rope_freqs(width):
    steps = jnp.arange(width // 2, dtype=jnp.float32)
    return jnp.exp(steps * (-2.0 * math.log(10000.0) / width))


def clip_of(frame_global, frames):
    ends = jnp.cumsum(frames)
    starts = ends - frames
    inside = (
        (frame_global[:, None] >= starts[None, :]) & (frame_global[:, None] < ends[None, :])
    ).astype(jnp.int32)
    clip_id = jnp.sum(inside * jnp.arange(frames.shape[0], dtype=jnp.int32)[None, :], axis=1)
    return (clip_id, inside, starts)


def rotary(token_index, frames, frame_rate, head_size):
    frame_global = token_index // FRAME
    clip_id, inside, starts = clip_of(frame_global, frames)
    frame_start = jnp.sum(inside * starts[None, :], axis=1)
    rate_token = jnp.sum(inside * frame_rate[None, :], axis=1).astype(jnp.float32)
    in_frame = token_index % FRAME
    time_pos = (frame_global - frame_start).astype(jnp.float32) * 24.0 / rate_token
    row_pos = (in_frame // GW).astype(jnp.float32)
    col_pos = (in_frame % GW).astype(jnp.float32)
    side = head_size // 6 * 2
    depth = head_size - 2 * side
    angles = jnp.concatenate(
        [
            time_pos[:, None] * rope_freqs(depth)[None, :],
            row_pos[:, None] * rope_freqs(side)[None, :],
            col_pos[:, None] * rope_freqs(side)[None, :],
        ],
        axis=1,
    )
    return (jnp.cos(angles), jnp.sin(angles))


def norm_rotate(rows, gain, cosine, sine):
    values_f = rows.astype(jnp.float32)
    mean_sq = jnp.mean(values_f * values_f, axis=-1, keepdims=True)
    normed = values_f * lax.rsqrt(mean_sq + 1e-06) * gain
    half = rows.shape[-1] // 2
    first, second = (normed[..., :half], normed[..., half:])
    cos_b = cosine[:, None, :]
    sin_b = sine[:, None, :]
    return jnp.concatenate(
        [first * cos_b - second * sin_b, second * cos_b + first * sin_b], axis=-1
    ).astype(jnp.bfloat16)


def kernel(cfg, q_ref, k_ref, v_ref, w_ref, mask_ref, out_ref,
           ka, va, kb, vb, wg, num, den, att, ptx, keep, rx1, stx, rx2, ytx, yrx,
           up_s, up_r, pt_s, pt_r, wu_s, wu_r, wd_s, wd_r, at_s, at_r,
           c_s, c_r, h_s, h_r, y_s, y_r, loc):
    n_out, reach, steps, q_cnt, heads, hs = cfg
    rows = q_ref.shape[0]
    pos = lax.axis_index("tm")
    head = lax.axis_index("head")
    o, b = pos // 2, pos % 2
    hi, lo = head // 2, head % 2
    partner = pos + 1 - 2 * b
    core = head + 1 - 2 * lo
    cross = lax.rem(head + 2, 4)
    has_up = o + 1 < n_out
    has_dn = o >= 1

    barrier = pltpu.get_barrier_semaphore()
    pl.semaphore_signal(barrier, inc=1, device_id={"tm": partner}, device_id_type=MESH)
    pl.semaphore_signal(barrier, inc=1, device_id={"head": core}, device_id_type=MESH)
    pl.semaphore_signal(barrier, inc=1, device_id={"head": cross}, device_id_type=MESH)

    @pl.when(has_up)
    def _():
        pl.semaphore_signal(barrier, inc=1, device_id={"tm": pos + 2}, device_id_type=MESH)

    @pl.when(has_dn)
    def _():
        pl.semaphore_signal(barrier, inc=1, device_id={"tm": pos - 2}, device_id_type=MESH)

    amount = 3 + has_up.astype(jnp.int32) + has_dn.astype(jnp.int32)
    pl.semaphore_wait(barrier, amount)

    def rcopy(src, dst, s, r, axis, index):
        return pltpu.make_async_remote_copy(
            src_ref=src, dst_ref=dst, send_sem=s, recv_sem=r,
            device_id={axis: index}, device_id_type=MESH)

    def a_ref(s):
        return (k_ref, v_ref) if s == 0 else (ka.at[s - 1], va.at[s - 1])

    def up_kv(s):
        src, dst = a_ref(s - 1), a_ref(s)
        return [rcopy(src[i], dst[i], up_s.at[s - 1, i], up_r.at[s - 1, i], "tm", pos + 2)
                for i in range(2)]

    def pair_kv(s):
        src, dst = a_ref(s), (kb.at[s], vb.at[s])
        return [rcopy(src[i], dst[i], pt_s.at[s, i], pt_r.at[s, i], "tm", partner)
                for i in range(2)]

    def needs(s):
        return (s >= 1 and 2 * s - 1 <= reach, 2 * s + 1 <= reach)

    def pair_gets(s):
        n0, n1 = needs(s)
        return (o >= s) & (((b == 0) & n0) | ((b == 1) & n1))

    def pair_sends(s):
        n0, n1 = needs(s)
        return (o >= s) & (((b == 1) & n0) | ((b == 0) & n1))

    def w_up(t):
        origin = jnp.maximum(o - t + 1, 0)
        return rcopy(wg.at[origin], wg.at[origin], wu_s.at[t - 1], wu_r.at[t - 1], "tm", pos + 2)

    def w_dn(t):
        origin = jnp.minimum(o + t - 1, n_out - 1)
        return rcopy(wg.at[origin], wg.at[origin], wd_s.at[t - 1], wd_r.at[t - 1], "tm", pos - 2)

    def start_all(cond, copies):
        @pl.when(cond)
        def _():
            for c in copies:
                c.start()

    def wait_recv(cond, copies):
        @pl.when(cond)
        def _():
            for c in copies:
                c.wait_recv()

    def wait_send(cond, copies):
        @pl.when(cond)
        def _():
            for c in copies:
                c.wait_send()

    def up_sends(t):
        return has_up & (o - t + 1 >= 0)

    def dn_sends(t):
        return has_dn & (o + t - 1 < n_out)

    scale = 1.0 / math.sqrt(hs)

    def attend(key_ref, value_ref, slot, first=False):
        mask = jnp.concatenate(
            [jnp.broadcast_to(mask_ref[slot, f:f + 1, :], (FRAME, rows))
             for f in range(rows // FRAME)], axis=0)

        def one(h, carry):
            at = pl.ds(pl.multiple_of(h * hs, hs), hs)
            scores = lax.dot_general(q_ref[:, at], key_ref[:, at], (((1,), (1,)), ((), ())),
                                     preferred_element_type=jnp.float32)
            probs = jnp.exp(scores * scale) * mask
            total = jnp.sum(probs, axis=1, keepdims=True)
            part = jnp.dot(probs.astype(jnp.bfloat16), value_ref[:, at],
                           preferred_element_type=jnp.float32)
            if first:
                den[h] = total
                num[:, at] = part
            else:
                den[h] += total
                num[:, at] += part
            return carry

        lax.fori_loop(0, heads, one, 0)

    start_all(has_up, up_kv(1))
    start_all(pair_sends(0), pair_kv(0))
    own = pltpu.make_async_copy(w_ref, wg.at[o], loc)
    own.start()
    own.wait()
    start_all(dn_sends(1), [w_dn(1)])
    attend(k_ref, v_ref, 0, first=True)

    def down(t):
        wait_recv(o + t < n_out, [w_dn(t)])
        if t + 1 < n_out:
            start_all(dn_sends(t + 1), [w_dn(t + 1)])

    def up(t):
        wait_recv(o - t >= 0, [w_up(t)])
        if t + 1 < n_out:
            start_all(up_sends(t + 1), [w_up(t + 1)])

    def use_pair(s):
        @pl.when(pair_gets(s))
        def _():
            for c in pair_kv(s):
                c.wait_recv()
            attend(kb.at[s], vb.at[s], steps + 1 + s)

    for s in range(1, steps + 1):
        if s < n_out:
            down(s)
        wait_recv(o >= s, up_kv(s))
        if s < steps:
            start_all(has_up & (o >= s), up_kv(s + 1))
        start_all(pair_sends(s), pair_kv(s))
        if s == max(steps - 1, 1):
            start_all(up_sends(1), [w_up(1)])
        if any(needs(s - 1)):
            use_pair(s - 1)
        if 2 * s <= reach:
            @pl.when(o >= s)
            def _():
                attend(*a_ref(s), s)
    for t in range(steps + 1, n_out):
        down(t)
    up(1)
    use_pair(steps)

    for h in range(heads):
        at = slice(h * hs, (h + 1) * hs)
        att[0:rows, at] = (num[:, at] / den[h]).astype(jnp.bfloat16)
    swap = rcopy(att.at[pl.ds(0, rows)], att.at[pl.ds(rows, rows)], at_s, at_r, "tm", partner)
    swap.start()
    for t in range(2, n_out):
        up(t)
    swap.wait_recv()

    def project(group, store):
        def one(k, carry):
            acc = None
            for h in range(heads):
                part = lax.dot_general(
                    att[:, h * hs:(h + 1) * hs], wg[group * q_cnt + k, h],
                    (((1,), (1,)), ((), ())), preferred_element_type=jnp.float32)
                acc = part if acc is None else acc + part
            store(k, acc)
            return carry
        if q_cnt == 1:
            one(0, 0)
        else:
            lax.fori_loop(0, q_cnt, one, 0)

    sides = (1 - hi, hi)
    c_copies = []
    for i, side in enumerate(sides):
        def put(k, acc, i=i):
            ptx[i, k] = acc.astype(jnp.bfloat16)
        project(2 * side + (1 - lo), put)
        copy = rcopy(ptx.at[i], rx1.at[i], c_s.at[i], c_r.at[i], "head", core)
        copy.start()
        c_copies.append(copy)
    for i, side in enumerate(sides):
        def put(k, acc, i=i):
            keep[i, k] = acc
        project(2 * side + lo, put)
    c_copies[0].wait_recv()
    h_copies = [None, None]
    for r in (1, 0):
        at = slice(r * rows, (r + 1) * rows)
        stx[r] = (keep[0, :, at] + rx1[0, :, at].astype(jnp.float32)).astype(jnp.bfloat16)
        h_copies[r] = rcopy(stx.at[r], rx2.at[r], h_s.at[r], h_r.at[r], "head", cross)
        h_copies[r].start()
    c_copies[1].wait_recv()

    def final(r):
        at = slice(r * rows, (r + 1) * rows)
        mine = keep[1, :, at] + rx1[1, :, at].astype(jnp.float32)
        return (mine + rx2[r].astype(jnp.float32)).astype(jnp.bfloat16)

    h_copies[1].wait_recv()
    ytx[...] = final(1)
    y_copy = rcopy(ytx, yrx, y_s, y_r, "tm", partner)
    y_copy.start()
    h_copies[0].wait_recv()
    out_ref[b] = final(0)
    y_copy.wait_recv()
    out_ref[1 - b] = yrx[...]

    for s in range(1, steps + 1):
        wait_send(has_up & (o >= s - 1), up_kv(s))
    for s in range(steps + 1):
        if any(needs(s)):
            wait_send(pair_sends(s), pair_kv(s))
    for t in range(1, n_out):
        wait_send(up_sends(t), [w_up(t)])
        wait_send(dn_sends(t), [w_dn(t)])
    for c in [swap, y_copy] + c_copies + h_copies:
        c.wait_send()


def per_device(queries, key_input, values, query_gain, key_gain, frames, frame_rate, out_weight):
    rows = queries.shape[0]
    hs = query_gain.shape[0]
    heads = queries.shape[1] // hs
    n = lax.axis_size("tm")
    m = lax.axis_size("head")
    n_out = n // 2
    per = rows // FRAME
    longest = n * per // 2
    back = min(WIN, longest) - 1
    reach = min((back + per - 1) // per, n - 1)
    steps = (reach + 1) // 2
    q_cnt = n_out // m
    dsl = out_weight.shape[1]

    pos = lax.axis_index("tm")
    b = pos % 2
    own_index = pos * rows + jnp.arange(rows, dtype=jnp.int32)
    cosine, sine = rotary(own_index, frames, frame_rate, hs)
    q_rot = norm_rotate(queries.reshape(rows, heads, hs), query_gain, cosine, sine)
    k_rot = norm_rotate(key_input.reshape(rows, heads, hs), key_gain, cosine, sine)

    back_by = jnp.stack([jnp.int32(2 * s) for s in range(steps + 1)]
                        + [2 * s + 2 * b - 1 for s in range(steps + 1)])
    q_frame = pos * per + jnp.arange(per, dtype=jnp.int32)
    q_clip = clip_of(q_frame, frames)[0]
    k_frame = ((pos - back_by)[:, None] * per
               + (jnp.arange(rows, dtype=jnp.int32) // FRAME)[None, :])
    k_clip = clip_of(k_frame.reshape(-1), frames)[0].reshape(k_frame.shape)
    kf, kc = k_frame[:, None, :], k_clip[:, None, :]
    qf, qc = q_frame[None, :, None], q_clip[None, :, None]
    mask = ((kf >= 0) & (kc == qc) & (kf <= qf) & (kf >= qf - (WIN - 1))).astype(jnp.float32)

    bf, f32 = jnp.bfloat16, jnp.float32
    width = heads * hs
    dma = pltpu.SemaphoreType.DMA
    out = pl.pallas_call(
        functools.partial(kernel, (n_out, reach, steps, q_cnt, heads, hs)),
        out_shape=jax.ShapeDtypeStruct((2, q_cnt, rows, dsl), bf),
        in_specs=[pl.BlockSpec(memory_space=pltpu.VMEM)] * 5,
        out_specs=pl.BlockSpec(memory_space=pltpu.VMEM),
        scratch_shapes=[
            pltpu.VMEM((steps, rows, width), bf),
            pltpu.VMEM((steps, rows, width), bf),
            pltpu.VMEM((steps + 1, rows, width), bf),
            pltpu.VMEM((steps + 1, rows, width), bf),
            pltpu.VMEM((n_out,) + out_weight.shape, bf),
            pltpu.VMEM((rows, width), f32),
            pltpu.VMEM((heads, rows, 1), f32),
            pltpu.VMEM((2 * rows, width), bf),
            pltpu.VMEM((2, q_cnt, 2 * rows, dsl), bf),
            pltpu.VMEM((2, q_cnt, 2 * rows, dsl), f32),
            pltpu.VMEM((2, q_cnt, 2 * rows, dsl), bf),
            pltpu.VMEM((2, q_cnt, rows, dsl), bf),
            pltpu.VMEM((2, q_cnt, rows, dsl), bf),
            pltpu.VMEM((q_cnt, rows, dsl), bf),
            pltpu.VMEM((q_cnt, rows, dsl), bf),
            dma((steps, 2)), dma((steps, 2)), dma((steps + 1, 2)), dma((steps + 1, 2)),
            dma((n_out - 1,)), dma((n_out - 1,)), dma((n_out - 1,)), dma((n_out - 1,)),
            dma, dma, dma((2,)), dma((2,)), dma((2,)), dma((2,)), dma, dma, dma,
        ],
        compiler_params=pltpu.CompilerParams(
            collective_id=0, has_side_effects=True, vmem_limit_bytes=56 * 1024 * 1024
        ),
    )(q_rot.reshape(rows, width), k_rot.reshape(rows, width), values, out_weight, mask)
    return jnp.transpose(out, (2, 1, 0, 3)).reshape(rows, 2 * q_cnt * dsl)


def solution(mesh):
    in_specs = (
        P("tm", "head"),
        P("tm", "head"),
        P("tm", "head"),
        P(),
        P(),
        P(),
        P(),
        P("head", "tm", None),
    )
    out_specs = P("tm", "head")
    return jax.shard_map(
        per_device, mesh=mesh, in_specs=in_specs, out_specs=out_specs, check_vma=False
    )
```

time: 229 us -> 104 us (0.45)
  the two profiles are of different devices: /device:TPU:0 before, /device:TPU:24 now
where the time goes in v1:
time: 104 us
  Pallas kernels  92.8 us (89%)
  local copies, waits for them, and re-layouts  8.17 us (8%)
  other arithmetic  2.57 us (2%)
    pallas_call x1, Pallas kernels, per_device(): pl.pallas_call(functools.partial(kernel, (n_out, reach, steps, q_cnt, hea...  92.8 us
    unnamed x12, local copies, waits for them, and re-layouts  4.16 us

profile of v1, /device:TPU:24, one launch (start us, length us, event | category | flops | bytes accessed | tf_op | source)
XLA Modules:
  0.0 103.7 jit_solution(15791212235176792968)
XLA Ops:
  0.0 1.2 %copy.15 = bf16[256,768]{0,1:T(8,128)(2,1)S(1)} copy(bf16[256,768]{1,0:T(8,128)(2,1)} %param.8) | data formatting | bytes 786432 | tf_op args[0]
  1.2 0.1 fusion
  1.3 0.9 copy-done
  2.2 0.2 copy.16
  2.3 0.1 fusion.2
  2.5 0.6 copy-done.1
  3.1 0.2 fusion.1
  3.5 0.6 copy-done.4
  4.2 0.2 reduce-window.8
  4.3 0.7 copy-done.3
  5.0 0.1 select_reduce_fusion.2
  5.1 0.1 broadcast_multiply_fusion.2
  5.2 0.2 fusion.5
  5.4 0.2 subtract_convert_fusion
  5.7 0.9 copy.17.q_ref
  6.6 0.9 copy.18.k_ref
  7.6 0.1 stack.15
  7.6 0.1 broadcast_compare_fusion
  7.8 0.1 select_reduce_fusion
  7.9 0.2 fusion.7
  8.1 0.7 and_convert_fusion.mask_ref
  8.8 92.8 %shard_map.82 = bf16[2,1,256,384]{3,2,1,0:T(8,128)(2,1)} custom-call(bf16[256,768]{1,0:T(8,128)(2,1)} %copy.17.q_ref, bf16[256,768]{1,0:T(8,128)(2,1)} %copy.18.k_ref, bf16[256,768]{1,0:T(8,128)(2,1)} %v_ref.1, bf16[6,384,128]{2,1,0:T(8,128)(2,1)} %w_ref.1, f32[6,2,256]{2,1,0:T(2,128)} %and_convert_fusion.mask_ref), custom_call_target="tpu_custom_call" | custom-call | tf_op jit(solution)/shard_map/pallas_call | solution.py:338
  101.6 1.2 %copy.19 = bf16[256,1,2,384]{0,3,2,1:T(8,128)(2,1)S(1)} copy(bf16[256,1,2,384]{3,0,1,2:T(8,128)(2,1)} %bitcast.21) | data formatting | bytes 786432 | tf_op jit(solution)/shard_map/transpose | solution.py:367
  102.8 0.9 copy.20
  (23 shorter events, 0.4 us)
Async XLA Ops:
  1.2 1.0 copy-start
  2.4 0.7 copy-start.1
  2.5 0.7 copy-start.2
  3.5 0.7 copy-start.4
  4.3 0.7 copy-start.3

commit v2 on v1

--- a/solution.py
+++ b/solution.py
@@ -65,8 +65,8 @@
 
 
 def kernel(cfg, q_ref, k_ref, v_ref, w_ref, mask_ref, out_ref,
-           ka, va, kb, vb, wg, num, den, att, ptx, keep, rx1, stx, rx2, ytx, yrx,
-           up_s, up_r, pt_s, pt_r, wu_s, wu_r, wd_s, wd_r, at_s, at_r,
+           qd, kb, vb, wg, num, den, ntx, nrx, dtx, drx, att, ptx, keep, rx1, stx, rx2, ytx, yrx,
+           qd_s, qd_r, pt_s, pt_r, nu_s, nu_r, wu_s, wu_r, wd_s, wd_r, at_s, at_r,
            c_s, c_r, h_s, h_r, y_s, y_r, loc):
     n_out, reach, steps, q_cnt, heads, hs = cfg
     rows = q_ref.shape[0]
@@ -101,29 +101,20 @@
             src_ref=src, dst_ref=dst, send_sem=s, recv_sem=r,
             device_id={axis: index}, device_id_type=MESH)
 
-    def a_ref(s):
-        return (k_ref, v_ref) if s == 0 else (ka.at[s - 1], va.at[s - 1])
-
-    def up_kv(s):
-        src, dst = a_ref(s - 1), a_ref(s)
-        return [rcopy(src[i], dst[i], up_s.at[s - 1, i], up_r.at[s - 1, i], "tm", pos + 2)
-                for i in range(2)]
-
-    def pair_kv(s):
-        src, dst = a_ref(s), (kb.at[s], vb.at[s])
-        return [rcopy(src[i], dst[i], pt_s.at[s, i], pt_r.at[s, i], "tm", partner)
-                for i in range(2)]
-
-    def needs(s):
-        return (s >= 1 and 2 * s - 1 <= reach, 2 * s + 1 <= reach)
-
-    def pair_gets(s):
-        n0, n1 = needs(s)
-        return (o >= s) & (((b == 0) & n0) | ((b == 1) & n1))
-
-    def pair_sends(s):
-        n0, n1 = needs(s)
-        return (o >= s) & (((b == 1) & n0) | ((b == 0) & n1))
+    def q_at(s):
+        return q_ref if s == 0 else qd.at[s - 1]
+
+    def q_dn(s):
+        return [rcopy(q_at(s - 1), q_at(s), qd_s.at[s - 1], qd_r.at[s - 1], "tm", pos - 2)]
+
+    def n_up(s):
+        return [rcopy(ntx.at[s - 1], nrx.at[s - 1], nu_s.at[s - 1, 0], nu_r.at[s - 1, 0],
+                      "tm", pos + 2),
+                rcopy(dtx.at[s - 1], drx.at[s - 1], nu_s.at[s - 1, 1], nu_r.at[s - 1, 1],
+                      "tm", pos + 2)]
+
+    pair_kv = [rcopy(k_ref, kb, pt_s.at[0], pt_r.at[0], "tm", partner),
+               rcopy(v_ref, vb, pt_s.at[1], pt_r.at[1], "tm", partner)]
 
     def w_up(t):
         origin = jnp.maximum(o - t + 1, 0)
@@ -157,38 +148,51 @@
     def dn_sends(t):
         return has_dn & (o + t - 1 < n_out)
 
+    def q_sends(s):
+        return has_dn & (o + s - 1 < n_out)
+
+    def n_sends(s):
+        return has_up & (o + s < n_out)
+
+    def n_gets(s):
+        return has_dn & (o + s < n_out)
+
     scale = 1.0 / math.sqrt(hs)
-
-    def attend(key_ref, value_ref, slot, first=False):
+    lane = lax.broadcasted_iota(jnp.int32, (rows, 128), 1)
+
+    def attend(s, key_ref, value_ref, slot, first):
+        query_ref = q_at(s)
         mask = jnp.concatenate(
             [jnp.broadcast_to(mask_ref[slot, f:f + 1, :], (FRAME, rows))
              for f in range(rows // FRAME)], axis=0)
+        if first:
+            den[s] = jnp.zeros((rows, 128), jnp.float32)
 
         def one(h, carry):
             at = pl.ds(pl.multiple_of(h * hs, hs), hs)
-            scores = lax.dot_general(q_ref[:, at], key_ref[:, at], (((1,), (1,)), ((), ())),
+            scores = lax.dot_general(query_ref[:, at], key_ref[:, at], (((1,), (1,)), ((), ())),
                                      preferred_element_type=jnp.float32)
             probs = jnp.exp(scores * scale) * mask
             total = jnp.sum(probs, axis=1, keepdims=True)
             part = jnp.dot(probs.astype(jnp.bfloat16), value_ref[:, at],
                            preferred_element_type=jnp.float32)
+            den[s] += jnp.where(lane == h, total, 0.0)
             if first:
-                den[h] = total
-                num[:, at] = part
+                num[s, :, at] = part
             else:
-                den[h] += total
-                num[:, at] += part
+                num[s, :, at] += part
             return carry
 
         lax.fori_loop(0, heads, one, 0)
 
-    start_all(has_up, up_kv(1))
-    start_all(pair_sends(0), pair_kv(0))
+    start_all(q_sends(1), q_dn(1))
+    for c in pair_kv:
+        c.start()
     own = pltpu.make_async_copy(w_ref, wg.at[o], loc)
     own.start()
     own.wait()
-    start_all(dn_sends(1), [w_dn(1)])
-    attend(k_ref, v_ref, 0, first=True)
+    start_all(up_sends(1), [w_up(1)])
+    attend(0, k_ref, v_ref, 0, True)
 
     def down(t):
         wait_recv(o + t < n_out, [w_dn(t)])
@@ -200,40 +204,64 @@
         if t + 1 < n_out:
             start_all(up_sends(t + 1), [w_up(t + 1)])
 
-    def use_pair(s):
-        @pl.when(pair_gets(s))
+    for s in range(1, steps + 1):
+        wait_recv(o + s < n_out, q_dn(s))
+        if s < steps:
+            start_all(q_sends(s + 1), q_dn(s + 1))
+        if s == max(steps - 1, 1):
+            start_all(dn_sends(1), [w_dn(1)])
+
+        @pl.when(o + s < n_out)
         def _():
-            for c in pair_kv(s):
-                c.wait_recv()
-            attend(kb.at[s], vb.at[s], steps + 1 + s)
-
-    for s in range(1, steps + 1):
-        if s < n_out:
-            down(s)
-        wait_recv(o >= s, up_kv(s))
+            attend(s, k_ref, v_ref, 2 * s, True)
+        if s == 1:
+            up(1)
+    for c in pair_kv:
+        c.wait_recv()
+
+    def with_pair(s):
+        cond = (o + s < n_out) & (((b == 0) & (s >= 1)) | ((b == 1) & (2 * s + 1 <= reach)))
+
+        @pl.when(cond)
+        def _():
+            attend(s, kb, vb, 2 * s + 1, False)
+
+    def add_up(s):
         if s < steps:
-            start_all(has_up & (o >= s), up_kv(s + 1))
-        start_all(pair_sends(s), pair_kv(s))
-        if s == max(steps - 1, 1):
-            start_all(up_sends(1), [w_up(1)])
-        if any(needs(s - 1)):
-            use_pair(s - 1)
-        if 2 * s <= reach:
-            @pl.when(o >= s)
+            @pl.when(n_gets(s))
             def _():
-                attend(*a_ref(s), s)
-    for t in range(steps + 1, n_out):
-        down(t)
-    up(1)
-    use_pair(steps)
+                for c in n_up(s + 1):
+                    c.wait_recv()
+                num[s] += nrx[s].astype(jnp.float32)
+                wide = jnp.concatenate(
+                    [drx[s], jnp.zeros((120, rows), jnp.float32)], axis=0)
+                den[s] += jnp.transpose(wide)
+        if s >= 1:
+            @pl.when(n_sends(s))
+            def _():
+                ntx[s - 1] = num[s].astype(jnp.bfloat16)
+                dtx[s - 1] = jnp.transpose(den[s])[0:8]
+                for c in n_up(s):
+                    c.start()
+
+    with_pair(steps)
+    add_up(steps)
+    for s in range(steps - 1, -1, -1):
+        with_pair(s)
+    up(2)
+    down(1)
+    for s in range(steps - 1, -1, -1):
+        add_up(s)
 
     for h in range(heads):
         at = slice(h * hs, (h + 1) * hs)
-        att[0:rows, at] = (num[:, at] / den[h]).astype(jnp.bfloat16)
+        att[0:rows, at] = (num[0, :, at] / den[0, :, h:h + 1]).astype(jnp.bfloat16)
     swap = rcopy(att.at[pl.ds(0, rows)], att.at[pl.ds(rows, rows)], at_s, at_r, "tm", partner)
     swap.start()
-    for t in range(2, n_out):
+    for t in range(3, n_out):
+        down(t - 1)
         up(t)
+    down(n_out - 1)
     swap.wait_recv()
 
     def project(group, store):
@@ -283,15 +311,21 @@
     y_copy = rcopy(ytx, yrx, y_s, y_r, "tm", partner)
     y_copy.start()
     h_copies[0].wait_recv()
-    out_ref[b] = final(0)
-    y_copy.wait_recv()
-    out_ref[1 - b] = yrx[...]
-
+    if len(out_ref.shape) == 2:
+        dsl = ytx.shape[-1]
+        out_ref[:, pl.ds(pl.multiple_of(b * dsl, 128), dsl)] = final(0)[0]
+        y_copy.wait_recv()
+        out_ref[:, pl.ds(pl.multiple_of((1 - b) * dsl, 128), dsl)] = yrx[0]
+    else:
+        out_ref[b] = final(0)
+        y_copy.wait_recv()
+        out_ref[1 - b] = yrx[...]
+
+    for c in pair_kv:
+        c.wait_send()
     for s in range(1, steps + 1):
-        wait_send(has_up & (o >= s - 1), up_kv(s))
-    for s in range(steps + 1):
-        if any(needs(s)):
-            wait_send(pair_sends(s), pair_kv(s))
+        wait_send(q_sends(s), q_dn(s))
+        wait_send(n_sends(s), n_up(s))
     for t in range(1, n_out):
         wait_send(up_sends(t), [w_up(t)])
         wait_send(dn_sends(t), [w_dn(t)])
@@ -321,33 +355,39 @@
     q_rot = norm_rotate(queries.reshape(rows, heads, hs), query_gain, cosine, sine)
     k_rot = norm_rotate(key_input.reshape(rows, heads, hs), key_gain, cosine, sine)
 
-    back_by = jnp.stack([jnp.int32(2 * s) for s in range(steps + 1)]
-                        + [2 * s + 2 * b - 1 for s in range(steps + 1)])
-    q_frame = pos * per + jnp.arange(per, dtype=jnp.int32)
-    q_clip = clip_of(q_frame, frames)[0]
-    k_frame = ((pos - back_by)[:, None] * per
+    frames_at = jnp.arange(per, dtype=jnp.int32)
+    q_pos = jnp.stack([pos + 2 * (slot // 2) for slot in range(2 * steps + 2)])
+    k_pos = jnp.stack([pos, pos + 1 - 2 * b] * (steps + 1))
+    q_frame = q_pos[:, None] * per + frames_at[None, :]
+    q_clip = clip_of(q_frame.reshape(-1), frames)[0].reshape(q_frame.shape)
+    k_frame = (k_pos[:, None] * per
                + (jnp.arange(rows, dtype=jnp.int32) // FRAME)[None, :])
     k_clip = clip_of(k_frame.reshape(-1), frames)[0].reshape(k_frame.shape)
     kf, kc = k_frame[:, None, :], k_clip[:, None, :]
-    qf, qc = q_frame[None, :, None], q_clip[None, :, None]
-    mask = ((kf >= 0) & (kc == qc) & (kf <= qf) & (kf >= qf - (WIN - 1))).astype(jnp.float32)
+    qf, qc = q_frame[:, :, None], q_clip[:, :, None]
+    mask = ((kc == qc) & (kf <= qf) & (kf >= qf - (WIN - 1))).astype(jnp.float32)
 
     bf, f32 = jnp.bfloat16, jnp.float32
     width = heads * hs
+    flat = q_cnt == 1 and dsl % 128 == 0
+    shape = (rows, 2 * dsl) if flat else (2, q_cnt, rows, dsl)
     dma = pltpu.SemaphoreType.DMA
     out = pl.pallas_call(
         functools.partial(kernel, (n_out, reach, steps, q_cnt, heads, hs)),
-        out_shape=jax.ShapeDtypeStruct((2, q_cnt, rows, dsl), bf),
+        out_shape=jax.ShapeDtypeStruct(shape, bf),
         in_specs=[pl.BlockSpec(memory_space=pltpu.VMEM)] * 5,
         out_specs=pl.BlockSpec(memory_space=pltpu.VMEM),
         scratch_shapes=[
             pltpu.VMEM((steps, rows, width), bf),
+            pltpu.VMEM((rows, width), bf),
+            pltpu.VMEM((rows, width), bf),
+            pltpu.VMEM((n_out,) + out_weight.shape, bf),
+            pltpu.VMEM((steps + 1, rows, width), f32),
+            pltpu.VMEM((steps + 1, rows, 128), f32),
             pltpu.VMEM((steps, rows, width), bf),
-            pltpu.VMEM((steps + 1, rows, width), bf),
-            pltpu.VMEM((steps + 1, rows, width), bf),
-            pltpu.VMEM((n_out,) + out_weight.shape, bf),
-            pltpu.VMEM((rows, width), f32),
-            pltpu.VMEM((heads, rows, 1), f32),
+            pltpu.VMEM((steps, rows, width), bf),
+            pltpu.VMEM((steps, 8, rows), f32),
+            pltpu.VMEM((steps, 8, rows), f32),
             pltpu.VMEM((2 * rows, width), bf),
             pltpu.VMEM((2, q_cnt, 2 * rows, dsl), bf),
             pltpu.VMEM((2, q_cnt, 2 * rows, dsl), f32),
@@ -356,7 +396,7 @@
             pltpu.VMEM((2, q_cnt, rows, dsl), bf),
             pltpu.VMEM((q_cnt, rows, dsl), bf),
             pltpu.VMEM((q_cnt, rows, dsl), bf),
-            dma((steps, 2)), dma((steps, 2)), dma((steps + 1, 2)), dma((steps + 1, 2)),
+            dma((steps,)), dma((steps,)), dma((2,)), dma((2,)), dma((steps, 2)), dma((steps, 2)),
             dma((n_out - 1,)), dma((n_out - 1,)), dma((n_out - 1,)), dma((n_out - 1,)),
             dma, dma, dma((2,)), dma((2,)), dma((2,)), dma((2,)), dma, dma, dma,
         ],
@@ -364,6 +404,8 @@
             collective_id=0, has_side_effects=True, vmem_limit_bytes=56 * 1024 * 1024
         ),
     )(q_rot.reshape(rows, width), k_rot.reshape(rows, width), values, out_weight, mask)
+    if flat:
+        return out
     return jnp.transpose(out, (2, 1, 0, 3)).reshape(rows, 2 * q_cnt * dsl)
 
 

time: 104 us -> 91 us (0.88)
  the two profiles are of different devices: /device:TPU:24 before, /device:TPU:0 now
where the time goes in v2:
time: 91 us; the launch traced here: 90.7 us
  Pallas kernels  80 us (88%)
  local copies, waits for them, and re-layouts  8.09 us (9%)
  other arithmetic  2.48 us (3%)
    pallas_call x1, Pallas kernels, per_device(): pl.pallas_call(functools.partial(kernel, (n_out, reach, steps, q_cnt, hea...  80 us
    unnamed x13, local copies, waits for them, and re-layouts  5.93 us
    convert_element_type x2, local copies, waits for them, and re-layouts, norm_rotate(): return jnp.concatenate([first * cos_b - second * sin_b, second * cos_b +...  1.83 us

profile of v2, /device:TPU:0, one launch (start us, length us, event | category | flops | bytes accessed | tf_op | source)
XLA Modules:
  0.0 90.7 jit_solution(5369515445748975110)
XLA Ops:
  0.0 1.2 %copy.13 = bf16[256,768]{0,1:T(8,128)(2,1)S(1)} copy(bf16[256,768]{1,0:T(8,128)(2,1)} %param.8) | data formatting | bytes 786432 | tf_op args[0]
  1.2 0.1 fusion
  1.3 0.9 copy-done
  2.2 0.2 copy.14
  2.3 0.1 fusion.2
  2.5 0.6 copy-done.1
  3.1 0.2 fusion.1
  3.5 0.6 copy-done.4
  4.2 0.2 reduce-window.8
  4.3 0.7 copy-done.3
  5.0 0.1 select_reduce_fusion.2
  5.2 0.2 fusion.5
  5.4 0.2 subtract_convert_fusion
  5.7 0.9 %copy.15.q_ref = bf16[256,768]{1,0:T(8,128)(2,1)} copy(bf16[256,768]{0,1:T(8,128)(2,1)S(1)} %bitcast.17) | data formatting | bytes 786432 | tf_op jit(solution)/shard_map/convert_element_type | solution.py:64
  6.6 0.9 %copy.16.k_ref = bf16[256,768]{1,0:T(8,128)(2,1)} copy(bf16[256,768]{0,1:T(8,128)(2,1)S(1)} %bitcast.18) | data formatting | bytes 786432 | tf_op jit(solution)/shard_map/convert_element_type | solution.py:64
  7.6 0.1 stack.31
  7.7 0.1 stack.28
  7.9 0.1 add.171
  8.0 0.1 select_reduce_fusion.3
  8.1 0.1 eq.24
  8.1 0.1 select_reduce_fusion
  8.3 0.7 and_convert_fusion.mask_ref
  8.9 80.0 %shard_map.82 = bf16[256,768]{1,0:T(8,128)(2,1)} custom-call(bf16[256,768]{1,0:T(8,128)(2,1)} %copy.15.q_ref, bf16[256,768]{1,0:T(8,128)(2,1)} %copy.16.k_ref, bf16[256,768]{1,0:T(8,128)(2,1)} %v_ref.1, bf16[6,384,128]{2,1,0:T(8,128)(2,1)} %w_ref.1, f32[6,2,256]{2,1,0:T(2,128)} %and_convert_fusion.mask_ref), custom_call_target="tpu_custom_call" | custom-call | tf_op jit(solution)/shard_map/pallas_call | solution.py:375
  89.0 1.8 %copy.18 = bf16[256,768]{1,0:T(8,128)(2,1)} copy(bf16[256,768]{1,0:T(8,128)(2,1)} %shard_map.82) | data formatting | bytes 786432
  (25 shorter events, 0.5 us)
Async XLA Ops:
  1.2 1.0 %copy-start = (bf16[256,768]{1,0:T(8,128)(2,1)S(1)}, bf16[256,768]{1,0:T(8,128)(2,1)}, u32[]{:S(2)}) copy-start(bf16[256,768]{1,0:T(8,128)(2,1)} %param.9) | copy-start | bytes 1179652
  2.4 0.7 copy-start.1
  2.5 0.7 copy-start.2
  3.5 0.7 copy-start.4
  4.3 0.7 copy-start.3

commit v3 on v2

--- a/solution.py
+++ b/solution.py
@@ -48,24 +48,12 @@
         ],
         axis=1,
     )
-    return (jnp.cos(angles), jnp.sin(angles))
-
-
-def norm_rotate(rows, gain, cosine, sine):
-    values_f = rows.astype(jnp.float32)
-    mean_sq = jnp.mean(values_f * values_f, axis=-1, keepdims=True)
-    normed = values_f * lax.rsqrt(mean_sq + 1e-06) * gain
-    half = rows.shape[-1] // 2
-    first, second = (normed[..., :half], normed[..., half:])
-    cos_b = cosine[:, None, :]
-    sin_b = sine[:, None, :]
-    return jnp.concatenate(
-        [first * cos_b - second * sin_b, second * cos_b + first * sin_b], axis=-1
-    ).astype(jnp.bfloat16)
-
-
-def kernel(cfg, q_ref, k_ref, v_ref, w_ref, mask_ref, out_ref,
-           qd, kb, vb, wg, num, den, ntx, nrx, dtx, drx, att, ptx, keep, rx1, stx, rx2, ytx, yrx,
+    cosine, sine = jnp.cos(angles), jnp.sin(angles)
+    return (jnp.concatenate([cosine, cosine], axis=1), jnp.concatenate([-sine, sine], axis=1))
+
+
+def kernel(cfg, q_hbm, k_hbm, v_hbm, w_hbm, cos_ref, sin_ref, gain_ref, mask_ref, out_ref,
+           q_ref, k_ref, v_ref, qd, kb, vb, wg, num, den, ntx, nrx, dtx, drx, att, ptx, keep, rx1, stx, rx2, ytx, yrx,
            qd_s, qd_r, pt_s, pt_r, nu_s, nu_r, wu_s, wu_r, wd_s, wd_r, at_s, at_r,
            c_s, c_r, h_s, h_r, y_s, y_r, loc):
     n_out, reach, steps, q_cnt, heads, hs = cfg
@@ -79,6 +67,11 @@
     cross = lax.rem(head + 2, 4)
     has_up = o + 1 < n_out
     has_dn = o >= 1
+
+    loads = [pltpu.make_async_copy(src, dst, loc.at[i]) for i, (src, dst) in enumerate(
+        [(w_hbm, wg.at[o]), (q_hbm, q_ref), (k_hbm, k_ref), (v_hbm, v_ref)])]
+    for c in loads:
+        c.start()
 
     barrier = pltpu.get_barrier_semaphore()
     pl.semaphore_signal(barrier, inc=1, device_id={"tm": partner}, device_id_type=MESH)
@@ -185,13 +178,26 @@
 
         lax.fori_loop(0, heads, one, 0)
 
+    def rotate(ref, row):
+        gain = gain_ref[row:row + 1, :]
+        for h in range(heads):
+            at = slice(h * hs, (h + 1) * hs)
+            x = ref[:, at].astype(jnp.float32)
+            mean_sq = jnp.mean(x * x, axis=1, keepdims=True)
+            x = x * lax.rsqrt(mean_sq + 1e-06) * gain
+            ref[:, at] = (x * cos_ref[...]
+                          + pltpu.roll(x, hs // 2, 1) * sin_ref[...]).astype(jnp.bfloat16)
+
+    loads[0].wait()
+    start_all(up_sends(1), [w_up(1)])
+    loads[3].wait()
+    pair_kv[1].start()
+    loads[1].wait()
+    rotate(q_ref, 0)
     start_all(q_sends(1), q_dn(1))
-    for c in pair_kv:
-        c.start()
-    own = pltpu.make_async_copy(w_ref, wg.at[o], loc)
-    own.start()
-    own.wait()
-    start_all(up_sends(1), [w_up(1)])
+    loads[2].wait()
+    rotate(k_ref, 1)
+    pair_kv[0].start()
     attend(0, k_ref, v_ref, 0, True)
 
     def down(t):
@@ -251,6 +257,8 @@
     up(2)
     down(1)
     for s in range(steps - 1, -1, -1):
+        if s == 0:
+            down(2)
         add_up(s)
 
     for h in range(heads):
@@ -259,9 +267,8 @@
     swap = rcopy(att.at[pl.ds(0, rows)], att.at[pl.ds(rows, rows)], at_s, at_r, "tm", partner)
     swap.start()
     for t in range(3, n_out):
-        down(t - 1)
+        down(t)
         up(t)
-    down(n_out - 1)
     swap.wait_recv()
 
     def project(group, store):
@@ -352,8 +359,7 @@
     b = pos % 2
     own_index = pos * rows + jnp.arange(rows, dtype=jnp.int32)
     cosine, sine = rotary(own_index, frames, frame_rate, hs)
-    q_rot = norm_rotate(queries.reshape(rows, heads, hs), query_gain, cosine, sine)
-    k_rot = norm_rotate(key_input.reshape(rows, heads, hs), key_gain, cosine, sine)
+    gains = jnp.stack([query_gain, key_gain])
 
     frames_at = jnp.arange(per, dtype=jnp.int32)
     q_pos = jnp.stack([pos + 2 * (slot // 2) for slot in range(2 * steps + 2)])
@@ -375,9 +381,13 @@
     out = pl.pallas_call(
         functools.partial(kernel, (n_out, reach, steps, q_cnt, heads, hs)),
         out_shape=jax.ShapeDtypeStruct(shape, bf),
-        in_specs=[pl.BlockSpec(memory_space=pltpu.VMEM)] * 5,
+        in_specs=[pl.BlockSpec(memory_space=pl.ANY)] * 4
+        + [pl.BlockSpec(memory_space=pltpu.VMEM)] * 4,
         out_specs=pl.BlockSpec(memory_space=pltpu.VMEM),
         scratch_shapes=[
+            pltpu.VMEM((rows, width), bf),
+            pltpu.VMEM((rows, width), bf),
+            pltpu.VMEM((rows, width), bf),
             pltpu.VMEM((steps, rows, width), bf),
             pltpu.VMEM((rows, width), bf),
             pltpu.VMEM((rows, width), bf),
@@ -398,12 +408,12 @@
             pltpu.VMEM((q_cnt, rows, dsl), bf),
             dma((steps,)), dma((steps,)), dma((2,)), dma((2,)), dma((steps, 2)), dma((steps, 2)),
             dma((n_out - 1,)), dma((n_out - 1,)), dma((n_out - 1,)), dma((n_out - 1,)),
-            dma, dma, dma((2,)), dma((2,)), dma((2,)), dma((2,)), dma, dma, dma,
+            dma, dma, dma((2,)), dma((2,)), dma((2,)), dma((2,)), dma, dma, dma((4,)),
         ],
         compiler_params=pltpu.CompilerParams(
             collective_id=0, has_side_effects=True, vmem_limit_bytes=56 * 1024 * 1024
         ),
-    )(q_rot.reshape(rows, width), k_rot.reshape(rows, width), values, out_weight, mask)
+    )(queries, key_input, values, out_weight, cosine, sine, gains, mask)
     if flat:
         return out
     return jnp.transpose(out, (2, 1, 0, 3)).reshape(rows, 2 * q_cnt * dsl)

time: 91 us -> 89.3 us (0.981)
  local copies, waits for them, and re-layouts: 8.09 us -> 4.08 us
  other arithmetic: 2.48 us -> 4.26 us
    unnamed x13 -> x9, local copies, waits for them, and re-layouts: 5.93 us -> 3.74 us
    convert_element_type x2 -> x0, local copies, waits for them, and re-layouts: 1.83 us -> none  [norm_rotate(): return jnp.concatenate([first * cos_b - second * sin_b, second * cos_b +...]
    concatenate x2, other arithmetic: 0.05 us -> 1.52 us  [the longest x1 0.76 us: rotary(): jnp.concatenate([cosine, cosine], axis=1)]
where the time goes in v3:
time: 89.3 us; the launch traced here: 89.1 us
  Pallas kernels  80.7 us (90%)
  other arithmetic  4.26 us (5%)
  local copies, waits for them, and re-layouts  4.08 us (5%)
    pallas_call x1, Pallas kernels, per_device(): pl.pallas_call(functools.partial(kernel, (n_out, reach, steps, q_cnt, hea...  80.7 us
    unnamed x9, local copies, waits for them, and re-layouts  3.74 us

profile of v3, /device:TPU:0, one launch (start us, length us, event | category | flops | bytes accessed | tf_op | source)
XLA Modules:
  0.0 89.1 jit_solution(8630572493957552545)
XLA Ops:
  0.0 0.0 copy-start.3
  0.0 0.6 copy-done.3
  0.7 0.2 reduce-window.8
  0.9 0.7 copy-done
  1.5 0.1 select_reduce_fusion.2
  1.6 0.1 broadcast_multiply_fusion.2
  1.8 0.1 broadcast_multiply_fusion.1
  1.9 0.6 fusion.5
  2.5 0.8 pad_maximum_fusion.2.sin_ref
  3.3 0.8 pad_maximum_fusion.1.cos_ref
  4.0 0.1 stack.40
  4.1 0.1 broadcast_add_fusion
  4.2 0.1 select_reduce_fusion
  4.3 0.1 stack.43
  4.4 0.1 iota_add_fusion
  4.5 0.1 add.145
  4.6 0.1 select_reduce_fusion.3
  4.6 0.1 eq.24
  4.7 0.7 and_convert_fusion.mask_ref
  5.4 0.7 copy-done.1
  6.1 0.0 copy-done.2
  6.1 0.6 pad_maximum_fusion.3.gain_ref
  6.6 80.7 %shard_map.82 = bf16[256,768]{1,0:T(8,128)(2,1)} custom-call(bf16[256,768]{1,0:T(8,128)(2,1)} %q_hbm.1, bf16[256,768]{1,0:T(8,128)(2,1)} %k_hbm.1, bf16[256,768]{1,0:T(8,128)(2,1)} %v_hbm.1, bf16[6,384,128]{2,1,0:T(8,128)(2,1)} %w_hbm.1, f32[256,128]{1,0:T(8,128)} %pad_maximum_fusion.1.cos_ref, f32[256,128]{1,0:T(8,128)} %pad_maximum_fusion.2.sin_ref, ...), custom_call_target="tpu_custom_call" | custom-call | tf_op jit(solution)/shard_map/pallas_call | solution.py:381
  87.4 1.8 %copy.10 = bf16[256,768]{1,0:T(8,128)(2,1)} copy(bf16[256,768]{1,0:T(8,128)(2,1)} %shard_map.82) | data formatting | bytes 786432
  (14 shorter events, 0.1 us)
Async XLA Ops:
  0.0 0.7 copy-start.3
  0.9 0.7 copy-start
  5.4 0.7 copy-start.1
  5.4 0.7 copy-start.2

commit v4 on v3

--- a/solution.py
+++ b/solution.py
@@ -266,7 +266,8 @@
         att[0:rows, at] = (num[0, :, at] / den[0, :, h:h + 1]).astype(jnp.bfloat16)
     swap = rcopy(att.at[pl.ds(0, rows)], att.at[pl.ds(rows, rows)], at_s, at_r, "tm", partner)
     swap.start()
-    for t in range(3, n_out):
+    last = n_out - 1
+    for t in range(3, last if q_cnt == 1 else n_out):
         down(t)
         up(t)
     swap.wait_recv()
@@ -286,47 +287,70 @@
         else:
             lax.fori_loop(0, q_cnt, one, 0)
 
-    sides = (1 - hi, hi)
-    c_copies = []
-    for i, side in enumerate(sides):
-        def put(k, acc, i=i):
-            ptx[i, k] = acc.astype(jnp.bfloat16)
-        project(2 * side + (1 - lo), put)
-        copy = rcopy(ptx.at[i], rx1.at[i], c_s.at[i], c_r.at[i], "head", core)
-        copy.start()
-        c_copies.append(copy)
-    for i, side in enumerate(sides):
-        def put(k, acc, i=i):
+    late = (o >= n_out // 2).astype(jnp.int32)
+    group = [i + late * (3 - 2 * i) for i in range(4)]
+    c_copies = [rcopy(ptx.at[p], rx1.at[p], c_s.at[p], c_r.at[p], "head", core) for p in range(2)]
+    h_copies = [rcopy(stx.at[r], rx2.at[r], h_s.at[r], h_r.at[r], "head", cross)
+                for r in range(2)]
+    y_copy = rcopy(ytx, yrx, y_s, y_r, "tm", partner)
+    mine = [(group[2 * p] // 2) == hi for p in range(2)]
+    dsl = ytx.shape[-1]
+
+    def partial(i):
+        def put(k, acc):
             keep[i, k] = acc
-        project(2 * side + lo, put)
-    c_copies[0].wait_recv()
-    h_copies = [None, None]
-    for r in (1, 0):
-        at = slice(r * rows, (r + 1) * rows)
-        stx[r] = (keep[0, :, at] + rx1[0, :, at].astype(jnp.float32)).astype(jnp.bfloat16)
-        h_copies[r] = rcopy(stx.at[r], rx2.at[r], h_s.at[r], h_r.at[r], "head", cross)
-        h_copies[r].start()
-    c_copies[1].wait_recv()
-
-    def final(r):
-        at = slice(r * rows, (r + 1) * rows)
-        mine = keep[1, :, at] + rx1[1, :, at].astype(jnp.float32)
-        return (mine + rx2[r].astype(jnp.float32)).astype(jnp.bfloat16)
-
-    h_copies[1].wait_recv()
-    ytx[...] = final(1)
-    y_copy = rcopy(ytx, yrx, y_s, y_r, "tm", partner)
-    y_copy.start()
-    h_copies[0].wait_recv()
-    if len(out_ref.shape) == 2:
-        dsl = ytx.shape[-1]
-        out_ref[:, pl.ds(pl.multiple_of(b * dsl, 128), dsl)] = final(0)[0]
-        y_copy.wait_recv()
-        out_ref[:, pl.ds(pl.multiple_of((1 - b) * dsl, 128), dsl)] = yrx[0]
-    else:
-        out_ref[b] = final(0)
-        y_copy.wait_recv()
-        out_ref[1 - b] = yrx[...]
+        project(group[i], put)
+
+        @pl.when(group[i] % 2 != lo)
+        def _():
+            ptx[i // 2] = keep[i].astype(jnp.bfloat16)
+            c_copies[i // 2].start()
+
+    def kept(p, at):
+        i = 2 * p + lax.rem(lo + late, 2)
+        return keep[i, :, at] + rx1[p, :, at].astype(jnp.float32)
+
+    def give(p):
+        c_copies[p].wait_recv()
+
+        @pl.when(jnp.logical_not(mine[p]))
+        def _():
+            for r in (1, 0):
+                stx[r] = kept(p, slice(r * rows, (r + 1) * rows)).astype(jnp.bfloat16)
+                h_copies[r].start()
+
+    def place(which, block):
+        if len(out_ref.shape) == 2:
+            out_ref[:, pl.ds(pl.multiple_of(which * dsl, 128), dsl)] = block[0]
+        else:
+            out_ref[which] = block
+
+    def finish(p):
+        @pl.when(mine[p])
+        def _():
+            for r in (1, 0):
+                h_copies[r].wait_recv()
+                total = (kept(p, slice(r * rows, (r + 1) * rows))
+                         + rx2[r].astype(jnp.float32)).astype(jnp.bfloat16)
+                if r == 1:
+                    ytx[...] = total
+                    y_copy.start()
+                else:
+                    place(b, total)
+
+    partial(0)
+    partial(1)
+    partial(2)
+    give(0)
+    if q_cnt == 1:
+        down(last)
+        up(last)
+    partial(3)
+    finish(0)
+    give(1)
+    finish(1)
+    y_copy.wait_recv()
+    place(1 - b, yrx[...])
 
     for c in pair_kv:
         c.wait_send()
@@ -400,7 +424,7 @@
             pltpu.VMEM((steps, 8, rows), f32),
             pltpu.VMEM((2 * rows, width), bf),
             pltpu.VMEM((2, q_cnt, 2 * rows, dsl), bf),
-            pltpu.VMEM((2, q_cnt, 2 * rows, dsl), f32),
+            pltpu.VMEM((4, q_cnt, 2 * rows, dsl), f32),
             pltpu.VMEM((2, q_cnt, 2 * rows, dsl), bf),
             pltpu.VMEM((2, q_cnt, rows, dsl), bf),
             pltpu.VMEM((2, q_cnt, rows, dsl), bf),

time: 89.3 us -> 93.3 us (1.045)
  the two profiles are of different devices: /device:TPU:0 before, /device:TPU:14 now
where the time goes in v4:
time: 93.3 us; the launch traced here: 93.1 us
  Pallas kernels  84.7 us (91%)
  other arithmetic  4.26 us (5%)
  local copies, waits for them, and re-layouts  4.08 us (4%)
    pallas_call x1, Pallas kernels, per_device(): pl.pallas_call(functools.partial(kernel, (n_out, reach, steps, q_cnt, hea...  84.7 us
    unnamed x9, local copies, waits for them, and re-layouts  3.74 us

profile of v4, /device:TPU:14, one launch (start us, length us, event | category | flops | bytes accessed | tf_op | source)
XLA Modules:
  0.0 93.1 jit_solution(8850264420554343828)
XLA Ops:
  0.0 0.0 copy-start.3
  0.0 0.6 copy-done.3
  0.7 0.2 reduce-window.8
  0.9 0.7 copy-done
  1.5 0.1 select_reduce_fusion.2
  1.6 0.1 broadcast_multiply_fusion.2
  1.8 0.1 broadcast_multiply_fusion.1
  1.9 0.6 fusion.5
  2.5 0.8 pad_maximum_fusion.2.sin_ref
  3.3 0.8 pad_maximum_fusion.1.cos_ref
  4.0 0.1 stack.40
  4.1 0.1 broadcast_add_fusion
  4.2 0.1 select_reduce_fusion
  4.3 0.1 stack.43
  4.4 0.1 iota_add_fusion
  4.5 0.1 add.145
  4.6 0.1 select_reduce_fusion.3
  4.6 0.1 eq.24
  4.7 0.7 and_convert_fusion.mask_ref
  5.4 0.7 copy-done.1
  6.1 0.0 copy-done.2
  6.1 0.6 pad_maximum_fusion.3.gain_ref
  6.6 84.7 %shard_map.82 = bf16[256,768]{1,0:T(8,128)(2,1)} custom-call(bf16[256,768]{1,0:T(8,128)(2,1)} %q_hbm.1, bf16[256,768]{1,0:T(8,128)(2,1)} %k_hbm.1, bf16[256,768]{1,0:T(8,128)(2,1)} %v_hbm.1, bf16[6,384,128]{2,1,0:T(8,128)(2,1)} %w_hbm.1, f32[256,128]{1,0:T(8,128)} %pad_maximum_fusion.1.cos_ref, f32[256,128]{1,0:T(8,128)} %pad_maximum_fusion.2.sin_ref, ...), custom_call_target="tpu_custom_call" | custom-call | tf_op jit(solution)/shard_map/pallas_call | solution.py:405
  91.4 1.8 %copy.10 = bf16[256,768]{1,0:T(8,128)(2,1)} copy(bf16[256,768]{1,0:T(8,128)(2,1)} %shard_map.82) | data formatting | bytes 786432
  (14 shorter events, 0.1 us)
Async XLA Ops:
  0.0 0.7 copy-start.3
  0.9 0.7 copy-start
  5.4 0.7 copy-start.1
  5.4 0.7 copy-start.2

commit v5 on v3

--- a/solution.py
+++ b/solution.py
@@ -176,7 +176,7 @@
                 num[s, :, at] += part
             return carry
 
-        lax.fori_loop(0, heads, one, 0)
+        lax.fori_loop(0, heads, one, 0, unroll=True)
 
     def rotate(ref, row):
         gain = gain_ref[row:row + 1, :]

time: 89.3 us -> 89.3 us (level)
  no operation moved by 1% of the time
where the time goes in v5:
time: 89.3 us; the launch traced here: 89.1 us
  Pallas kernels  80.7 us (90%)
  other arithmetic  4.26 us (5%)
  local copies, waits for them, and re-layouts  4.08 us (5%)
    pallas_call x1, Pallas kernels, per_device(): pl.pallas_call(functools.partial(kernel, (n_out, reach, steps, q_cnt, hea...  80.7 us
    unnamed x9, local copies, waits for them, and re-layouts  3.74 us

profile of v5, /device:TPU:0, one launch (start us, length us, event | category | flops | bytes accessed | tf_op | source)
XLA Modules:
  0.0 89.1 jit_solution(2114390540242897351)
XLA Ops:
  0.0 0.0 copy-start.3
  0.0 0.6 copy-done.3
  0.7 0.2 reduce-window.8
  0.9 0.7 copy-done
  1.5 0.1 select_reduce_fusion.2
  1.6 0.1 broadcast_multiply_fusion.2
  1.8 0.1 broadcast_multiply_fusion.1
  1.9 0.6 fusion.5
  2.5 0.8 pad_maximum_fusion.2.sin_ref
  3.3 0.8 pad_maximum_fusion.1.cos_ref
  4.0 0.1 stack.40
  4.1 0.1 broadcast_add_fusion
  4.2 0.1 select_reduce_fusion
  4.3 0.1 stack.43
  4.4 0.1 iota_add_fusion
  4.5 0.1 add.145
  4.6 0.1 select_reduce_fusion.3
  4.6 0.1 eq.24
  4.7 0.7 and_convert_fusion.mask_ref
  5.4 0.7 copy-done.1
  6.1 0.0 copy-done.2
  6.1 0.6 pad_maximum_fusion.3.gain_ref
  6.6 80.7 %shard_map.82 = bf16[256,768]{1,0:T(8,128)(2,1)} custom-call(bf16[256,768]{1,0:T(8,128)(2,1)} %q_hbm.1, bf16[256,768]{1,0:T(8,128)(2,1)} %k_hbm.1, bf16[256,768]{1,0:T(8,128)(2,1)} %v_hbm.1, bf16[6,384,128]{2,1,0:T(8,128)(2,1)} %w_hbm.1, f32[256,128]{1,0:T(8,128)} %pad_maximum_fusion.1.cos_ref, f32[256,128]{1,0:T(8,128)} %pad_maximum_fusion.2.sin_ref, ...), custom_call_target="tpu_custom_call" | custom-call | tf_op jit(solution)/shard_map/pallas_call | solution.py:381
  87.4 1.8 %copy.10 = bf16[256,768]{1,0:T(8,128)(2,1)} copy(bf16[256,768]{1,0:T(8,128)(2,1)} %shard_map.82) | data formatting | bytes 786432
  (14 shorter events, 0.1 us)
Async XLA Ops:
  0.0 0.7 copy-start.3
  0.9 0.7 copy-start
  5.4 0.7 copy-start.1
  5.4 0.7 copy-start.2

commit v6 on v3

--- a/solution.py
+++ b/solution.py
@@ -273,12 +273,9 @@
 
     def project(group, store):
         def one(k, carry):
-            acc = None
-            for h in range(heads):
-                part = lax.dot_general(
-                    att[:, h * hs:(h + 1) * hs], wg[group * q_cnt + k, h],
-                    (((1,), (1,)), ((), ())), preferred_element_type=jnp.float32)
-                acc = part if acc is None else acc + part
+            weight = jnp.concatenate([wg[group * q_cnt + k, h] for h in range(heads)], axis=1)
+            acc = lax.dot_general(att[...], weight, (((1,), (1,)), ((), ())),
+                                  preferred_element_type=jnp.float32)
             store(k, acc)
             return carry
         if q_cnt == 1:

time: 89.3 us -> 88.6 us (level)
  no operation moved by 1% of the time
where the time goes in v6:
time: 88.6 us; the launch traced here: 88.4 us
  Pallas kernels  80 us (90%)
  other arithmetic  4.26 us (5%)
  local copies, waits for them, and re-layouts  4.08 us (5%)
    pallas_call x1, Pallas kernels, per_device(): pl.pallas_call(functools.partial(kernel, (n_out, reach, steps, q_cnt, hea...  80 us
    unnamed x9, local copies, waits for them, and re-layouts  3.74 us

profile of v6, /device:TPU:0, one launch (start us, length us, event | category | flops | bytes accessed | tf_op | source)
XLA Modules:
  0.0 88.4 jit_solution(17488081800976983985)
XLA Ops:
  0.0 0.0 copy-start.3
  0.0 0.6 copy-done.3
  0.7 0.2 reduce-window.8
  0.9 0.7 copy-done
  1.5 0.1 select_reduce_fusion.2
  1.6 0.1 broadcast_multiply_fusion.2
  1.8 0.1 broadcast_multiply_fusion.1
  1.9 0.6 fusion.5
  2.5 0.8 pad_maximum_fusion.2.sin_ref
  3.3 0.8 pad_maximum_fusion.1.cos_ref
  4.0 0.1 stack.40
  4.1 0.1 broadcast_add_fusion
  4.2 0.1 select_reduce_fusion
  4.3 0.1 stack.43
  4.4 0.1 iota_add_fusion
  4.5 0.1 add.145
  4.6 0.1 select_reduce_fusion.3
  4.6 0.1 eq.24
  4.7 0.7 and_convert_fusion.mask_ref
  5.4 0.7 copy-done.1
  6.1 0.0 copy-done.2
  6.1 0.6 pad_maximum_fusion.3.gain_ref
  6.6 80.0 %shard_map.82 = bf16[256,768]{1,0:T(8,128)(2,1)} custom-call(bf16[256,768]{1,0:T(8,128)(2,1)} %q_hbm.1, bf16[256,768]{1,0:T(8,128)(2,1)} %k_hbm.1, bf16[256,768]{1,0:T(8,128)(2,1)} %v_hbm.1, bf16[6,384,128]{2,1,0:T(8,128)(2,1)} %w_hbm.1, f32[256,128]{1,0:T(8,128)} %pad_maximum_fusion.1.cos_ref, f32[256,128]{1,0:T(8,128)} %pad_maximum_fusion.2.sin_ref, ...), custom_call_target="tpu_custom_call" | custom-call | tf_op jit(solution)/shard_map/pallas_call | solution.py:378
  86.6 1.8 %copy.10 = bf16[256,768]{1,0:T(8,128)(2,1)} copy(bf16[256,768]{1,0:T(8,128)(2,1)} %shard_map.82) | data formatting | bytes 786432
  (14 shorter events, 0.1 us)
Async XLA Ops:
  0.0 0.7 copy-start.3
  0.9 0.7 copy-start
  5.4 0.7 copy-start.1
  5.4 0.7 copy-start.2

commit v7 on v6

--- a/solution.py
+++ b/solution.py
@@ -195,6 +195,7 @@
     loads[1].wait()
     rotate(q_ref, 0)
     start_all(q_sends(1), q_dn(1))
+    start_all(dn_sends(1), [w_dn(1)])
     loads[2].wait()
     rotate(k_ref, 1)
     pair_kv[0].start()
@@ -214,8 +215,6 @@
         wait_recv(o + s < n_out, q_dn(s))
         if s < steps:
             start_all(q_sends(s + 1), q_dn(s + 1))
-        if s == max(steps - 1, 1):
-            start_all(dn_sends(1), [w_dn(1)])
 
         @pl.when(o + s < n_out)
         def _():

time: 88.6 us -> 94.4 us (1.065)
  Pallas kernels: 80 us -> 85.8 us
    pallas_call x1, Pallas kernels: 80 us -> 85.8 us  [per_device(): pl.pallas_call(functools.partial(kernel, (n_out, reach, steps, q_cnt, hea...]
where the time goes in v7:
time: 94.4 us; the launch traced here: 94.2 us
  Pallas kernels  85.8 us (91%)
  other arithmetic  4.26 us (5%)
  local copies, waits for them, and re-layouts  4.08 us (4%)
    pallas_call x1, Pallas kernels, per_device(): pl.pallas_call(functools.partial(kernel, (n_out, reach, steps, q_cnt, hea...  85.8 us
    unnamed x9, local copies, waits for them, and re-layouts  3.74 us

profile of v7, /device:TPU:0, one launch (start us, length us, event | category | flops | bytes accessed | tf_op | source)
XLA Modules:
  0.0 94.2 jit_solution(11864186387289234140)
XLA Ops:
  0.0 0.0 copy-start.3
  0.0 0.6 copy-done.3
  0.7 0.2 reduce-window.8
  0.9 0.7 copy-done
  1.5 0.1 select_reduce_fusion.2
  1.6 0.1 broadcast_multiply_fusion.2
  1.8 0.1 broadcast_multiply_fusion.1
  1.9 0.6 fusion.5
  2.5 0.8 pad_maximum_fusion.2.sin_ref
  3.3 0.8 pad_maximum_fusion.1.cos_ref
  4.0 0.1 stack.40
  4.1 0.1 broadcast_add_fusion
  4.2 0.1 select_reduce_fusion
  4.3 0.1 stack.43
  4.4 0.1 iota_add_fusion
  4.5 0.1 add.145
  4.6 0.1 select_reduce_fusion.3
  4.6 0.1 eq.24
  4.7 0.7 and_convert_fusion.mask_ref
  5.4 0.7 copy-done.1
  6.1 0.0 copy-done.2
  6.1 0.6 pad_maximum_fusion.3.gain_ref
  6.6 85.8 %shard_map.82 = bf16[256,768]{1,0:T(8,128)(2,1)} custom-call(bf16[256,768]{1,0:T(8,128)(2,1)} %q_hbm.1, bf16[256,768]{1,0:T(8,128)(2,1)} %k_hbm.1, bf16[256,768]{1,0:T(8,128)(2,1)} %v_hbm.1, bf16[6,384,128]{2,1,0:T(8,128)(2,1)} %w_hbm.1, f32[256,128]{1,0:T(8,128)} %pad_maximum_fusion.1.cos_ref, f32[256,128]{1,0:T(8,128)} %pad_maximum_fusion.2.sin_ref, ...), custom_call_target="tpu_custom_call" | custom-call | tf_op jit(solution)/shard_map/pallas_call | solution.py:377
  92.5 1.8 %copy.10 = bf16[256,768]{1,0:T(8,128)(2,1)} copy(bf16[256,768]{1,0:T(8,128)(2,1)} %shard_map.82) | data formatting | bytes 786432
  (14 shorter events, 0.1 us)
Async XLA Ops:
  0.0 0.7 copy-start.3
  0.9 0.7 copy-start
  5.4 0.7 copy-start.1
  5.4 0.7 copy-start.2
